TPU v7x, 256 devices: a whole 4x4x8 slice. The times are simulated.
256 devices in a mesh: tm: 8 (over z), height: 16 (over x, y), cam: 2 (over core).
Axes of the slice: x: 4, y: 4, z: 8, core: 2. Of those that a mesh axis runs over, the one named last changes fastest.
Arguments:
- video_clip: bfloat16 [2, 32, 128, 64, 256], P('cam', 'tm', 'height'), may hold values from -6 to 6
- valid_from: int32 [2], P('cam'), may hold values from 0 to 16, as said below
- norm_gain: float32 [256], replicated, may hold values from 0.5 to 1.5
- spatial_weight: bfloat16 [3, 3, 256, 256], replicated, may hold values from -0.125 to 0.125
- temporal_weight: bfloat16 [3, 256, 256], replicated, may hold values from -0.21875 to 0.21875
- mix_weight: bfloat16 [3, 256, 256], replicated, may hold values from -0.21875 to 0.21875
- cotangent: bfloat16 [2, 16, 128, 64, 256], P('cam', None, ('height', 'tm')), may hold values from -6 to 6
Outputs:
- encoded: bfloat16 [2, 16, 128, 64, 256], P('cam', None, ('height', 'tm'))
- video_gradient: bfloat16 [2, 32, 128, 64, 256], P('cam', 'tm', 'height')
- spatial_gradient: float32 [3, 3, 256, 256], replicated
- temporal_gradient: float32 [3, 256, 256], replicated
- mix_gradient: float32 [3, 256, 256], replicated
- gain_gradient: float32 [256], replicated
Inputs may be any that keep to these rules, and one draw needn't show every extreme that they name: Frames before valid_from of a camera are padding. In every draw some camera starts at 16.
All inputs are finite; a program needn't handle non-finite values.
Results may differ from a plain program's by a relative error of at most 0.0065.
Values may be sent and summed in bfloat16 or wider, within the bound.
A program may use at most 128 MiB of HBM per device.

v0:
```python
import math
import jax
import jax.numpy as jnp
from jax import lax
from jax.sharding import PartitionSpec as P


def extended(array, sides, width):
    for axis, dim in sides:
        size, length = (lax.axis_size(axis), array.shape[dim])
        up = [(i, (i + 1) % size) for i in range(size - 1)]
        down = [(j, i) for i, j in up]
        last = lax.slice_in_dim(array, length - width, length, axis=dim)
        initial = lax.slice_in_dim(array, 0, width, axis=dim)
        before = lax.ppermute(last, axis, up)
        after = lax.ppermute(initial, axis, down)
        array = jnp.concatenate([before, array, after], axis=dim)
    return array


def shifted(block, axis, distance):
    devices = range(lax.axis_size(axis))
    route = [(i - distance, i) for i in devices if i - distance in devices]
    return lax.ppermute(block, axis, route)


def project(rows_in, weight):
    flat_rows = rows_in.reshape(-1, rows_in.shape[-1])
    product = jnp.dot(flat_rows, weight, preferred_element_type=jnp.float32)
    return product.reshape(rows_in.shape[:-1] + (weight.shape[-1],))


def project_back(rows_in, weight):
    flat_rows = rows_in.reshape(-1, rows_in.shape[-1])
    product = lax.dot_general(
        flat_rows, weight, (((1,), (1,)), ((), ())), preferred_element_type=jnp.float32
    )
    return product.reshape(rows_in.shape[:-1] + (weight.shape[0],))


def outer_sum(left_rows, right_rows):
    return lax.dot_general(
        left_rows.reshape(-1, left_rows.shape[-1]),
        right_rows.reshape(-1, right_rows.shape[-1]),
        (((0,), (0,)), ((), ())),
        preferred_element_type=jnp.float32,
    )


def column_pad(padded):
    return jnp.pad(padded, ((0, 0), (0, 0), (0, 0), (1, 1), (0, 0)))


def spatial(padded, weight):
    columns = column_pad(padded)
    rows_here = padded.shape[2] - 2
    width_here = padded.shape[3]
    accumulated = jnp.zeros(
        padded.shape[:2] + (rows_here, width_here, weight.shape[-1]), jnp.float32
    )
    for row_tap in range(3):
        for column_tap in range(3):
            window = columns[
                :, :, row_tap : row_tap + rows_here, column_tap : column_tap + width_here
            ]
            accumulated = accumulated + project(window, weight[row_tap, column_tap])
    return accumulated


def spatial_grad(padded, gradient):
    columns = column_pad(padded)
    rows_here = padded.shape[2] - 2
    width_here = padded.shape[3]
    outer_rows = []
    for row_tap in range(3):
        inner_rows = []
        for column_tap in range(3):
            window = columns[
                :, :, row_tap : row_tap + rows_here, column_tap : column_tap + width_here
            ]
            inner_rows.append(outer_sum(window, gradient))
        outer_rows.append(jnp.stack(inner_rows))
    return jnp.stack(outer_rows)


def flipped(weight):
    return jnp.transpose(weight[::-1, ::-1], (0, 1, 3, 2))


def norm_forward(masked, norm_gain):
    values = masked.astype(jnp.float32)
    inverse = lax.rsqrt(jnp.mean(values * values, axis=-1, keepdims=True) + 1e-06)
    unit_rows = values * inverse
    return ((unit_rows * norm_gain).astype(jnp.bfloat16), unit_rows, inverse)


def norm_backward(normed_gradient, unit_rows, inverse, norm_gain, present):
    unit_gradient = normed_gradient * norm_gain
    masked_gradient = inverse * (
        unit_gradient - unit_rows * jnp.mean(unit_gradient * unit_rows, axis=-1, keepdims=True)
    )
    video_gradient = jnp.where(present, masked_gradient, jnp.zeros_like(masked_gradient)).astype(
        jnp.bfloat16
    )
    gain_gradient = jnp.sum((normed_gradient * unit_rows).reshape(-1, unit_rows.shape[-1]), axis=0)
    return (video_gradient, gain_gradient)


def split_frames(active, prior_frame):
    dims_in = active.shape
    frame_pairs = active.reshape(dims_in[0], dims_in[1] // 2, 2, dims_in[2], dims_in[3], dims_in[4])
    even_frames = frame_pairs[:, :, 0]
    odd_frames = frame_pairs[:, :, 1]
    prior_odd = jnp.concatenate([prior_frame, odd_frames[:, :-1]], axis=1)
    return (even_frames, odd_frames, prior_odd)


def temporal_forward(even_frames, odd_frames, prior_odd, weight):
    accumulated = (
        project(odd_frames, weight[0])
        + project(even_frames, weight[1])
        + project(prior_odd, weight[2])
    )
    return accumulated.astype(jnp.bfloat16)


def temporal_backward(even_frames, odd_frames, prior_odd, strided_gradient, following, weight):
    weight_gradient = jnp.stack(
        [
            outer_sum(odd_frames, strided_gradient),
            outer_sum(even_frames, strided_gradient),
            outer_sum(prior_odd, strided_gradient),
        ]
    )
    next_gradient = jnp.concatenate([strided_gradient[:, 1:], following], axis=1)
    odd_gradient = project_back(strided_gradient, weight[0]) + project_back(
        next_gradient, weight[2]
    )
    even_gradient = project_back(strided_gradient, weight[1])
    dims_in = even_frames.shape
    active_gradient = jnp.stack([even_gradient, odd_gradient], axis=2).reshape(
        dims_in[0], dims_in[1] * 2, dims_in[2], dims_in[3], dims_in[4]
    )
    return (active_gradient, weight_gradient)


def mix_forward(regrouped, weight):
    frame_count = regrouped.shape[1]
    blank_frames = jnp.zeros(regrouped.shape[:1] + (2,) + regrouped.shape[2:], regrouped.dtype)
    history = jnp.concatenate([blank_frames, regrouped], axis=1)
    accumulated = regrouped.astype(jnp.float32)
    for offset in range(3):
        accumulated = accumulated + project(
            history[:, 2 - offset : 2 - offset + frame_count], weight[offset]
        )
    return (accumulated.astype(jnp.bfloat16), history)


def mix_backward(history, cotangent, weight):
    frame_count = cotangent.shape[1]
    mix_gradient = jnp.stack(
        [
            outer_sum(history[:, 2 - offset : 2 - offset + frame_count], cotangent)
            for offset in range(3)
        ]
    )
    blank_frames = jnp.zeros(cotangent.shape[:1] + (2,) + cotangent.shape[2:], cotangent.dtype)
    ahead = jnp.concatenate([cotangent, blank_frames], axis=1)
    accumulated = cotangent.astype(jnp.float32)
    for offset in range(3):
        accumulated = accumulated + project_back(
            ahead[:, offset : offset + frame_count], weight[offset]
        )
    return (mix_gradient, accumulated.astype(jnp.bfloat16))


def activation_backward(active_gradient, pre_activation):
    sigmoid_value = jax.nn.sigmoid(pre_activation)
    return (
        active_gradient * sigmoid_value * (1.0 + pre_activation * (1.0 - sigmoid_value))
    ).astype(jnp.bfloat16)


def on_device(
    video_clip, valid_from, norm_gain, spatial_weight, temporal_weight, mix_weight, cotangent
):
    frames_here = video_clip.shape[1]
    frames = lax.axis_index("tm") * frames_here + jnp.arange(frames_here, dtype=jnp.int32)
    present = (frames[None, :] >= valid_from[:, None])[:, :, None, None, None]
    masked = jnp.where(present, video_clip, jnp.zeros_like(video_clip))
    normed, unit_rows, inverse = norm_forward(masked, norm_gain)
    padded = extended(normed, (("height", 2),), 1)
    pre_activation = spatial(padded, spatial_weight)
    active = jax.nn.silu(pre_activation).astype(jnp.bfloat16)
    prior_frame = shifted(active[:, frames_here - 1 :], "tm", 1)
    even_frames, odd_frames, prior_odd = split_frames(active, prior_frame)
    strided = temporal_forward(even_frames, odd_frames, prior_odd, temporal_weight)
    regrouped = lax.all_to_all(strided, "tm", split_axis=2, concat_axis=1, tiled=True)
    encoded, history = mix_forward(regrouped, mix_weight)
    mix_gradient, regrouped_gradient = mix_backward(history, cotangent, mix_weight)
    strided_gradient = lax.all_to_all(
        regrouped_gradient, "tm", split_axis=1, concat_axis=2, tiled=True
    )
    following = shifted(strided_gradient[:, :1], "tm", -1)
    active_gradient, temporal_gradient = temporal_backward(
        even_frames, odd_frames, prior_odd, strided_gradient, following, temporal_weight
    )
    pre_gradient = activation_backward(active_gradient, pre_activation)
    spatial_gradient = spatial_grad(padded, pre_gradient)
    gradient_padded = extended(pre_gradient, (("height", 2),), 1)
    normed_gradient = spatial(gradient_padded, flipped(spatial_weight))
    video_gradient, gain_gradient = norm_backward(
        normed_gradient, unit_rows, inverse, norm_gain, present
    )
    mix_gradient, temporal_gradient, spatial_gradient, gain_gradient = lax.psum(
        (mix_gradient, temporal_gradient, spatial_gradient, gain_gradient), ("tm", "height", "cam")
    )
    cell_count = (
        video_clip.shape[0]
        * lax.axis_size("cam")
        * frames_here
        * lax.axis_size("tm")
        * video_clip.shape[2]
        * lax.axis_size("height")
        * video_clip.shape[3]
    )
    gradient_scale = 1.0 / math.sqrt(cell_count)
    return (
        encoded,
        video_gradient,
        spatial_gradient * gradient_scale,
        temporal_gradient * gradient_scale,
        mix_gradient * gradient_scale,
        gain_gradient * gradient_scale,
    )


def solution(mesh):
    return jax.shard_map(
        on_device,
        mesh=mesh,
        in_specs=(
            P("cam", "tm", "height", None, None),
            P("cam"),
            P(),
            P(),
            P(),
            P(),
            P("cam", None, ("height", "tm"), None, None),
        ),
        out_specs=(
            P("cam", None, ("height", "tm"), None, None),
            P("cam", "tm", "height", None, None),
            P(),
            P(),
            P(),
            P(),
        ),
        check_vma=False,
    )
```

profile of v0, /device:TPU:2, one launch (start us, length us, event | category | flops | bytes accessed | tf_op | source)
XLA Modules:
  0.0 402.6 jit_solution(15002015680635062406)
XLA Ops:
  7.9 1.6 fusion.12
  9.6 1.6 fusion.5
  11.2 0.8 fusion.139
  12.0 3.5 collective-permute-start
  15.5 4.5 %collective-permute-start.1 = (bf16[1,4,1,64,256]{4,3,2,1,0:T(8,128)(2,1)}, bf16[1,4,1,64,256]{4,3,2,1,0:T(8,128)(2,1)S(1)}, u32[]{:S(2)}, u32[]{:S(2)}) collective-permute-start(bf16[1,4,1,64,256]{4,3,2,1,0:T(8,128)(2,1)} %get-tuple-element.43), channel_id=1, source_target_pairs={{2,0},{4,2},{6,4},{8,6},{10,8},{12,10},{14,12},{16,14},{18,16},{20... | collective-permute-start | bytes 393224 | tf_op jit(solution)/shard_map/ppermute | solution.py:16
  20.7 1.2 fusion.23
  21.8 8.5 %all-to-all-start.1 = ((bf16[1,16,1,64,256]{4,3,2,0,1:T(8,128)(2,1)}), bf16[1,16,1,64,256]{4,3,2,0,1:T(8,128)(2,1)S(1)}, u32[]{:S(2)}, u32[]{:S(2)}) async-start(bf16[1,16,1,64,256]{4,3,2,0,1:T(8,128)(2,1)} %fusion.23), calls=%async_computation.1 | async-start | bytes 1048576 | tf_op jit(solution)/shard_map/all_to_all | solution.py:201
  30.3 1.8 fusion.42
  32.1 1.5 copy.47
  33.6 2.5 reverse_bitcast_fusion
  36.1 0.8 select_maximum_fusion.2
  36.9 1.8 fusion.44
  38.7 1.8 fusion.45
  40.5 1.8 fusion.46
  42.3 1.9 fusion.51
  44.2 1.8 fusion.47
  46.0 1.7 fusion.48
  47.7 1.8 fusion.49
  49.5 0.8 copy-done.5
  50.3 1.2 copy.91
  51.6 1.3 collective-permute-start.3
  53.6 7.1 %collective-permute-done.3 = bf16[1,1,8,64,256]{4,3,2,1,0:T(8,128)(2,1)S(1)} collective-permute-done((bf16[1,1,8,64,256]{4,3,2,1,0:T(8,128)(2,1)S(1)}, bf16[1,1,8,64,256]{4,3,2,1,0:T(8,128)(2,1)S(1)}, u32[]{:S(2)}, u32[]{:S(2)}) %collective-permute-start.3) | collective-permute-done | bytes 262176 | tf_op jit(solution)/shard_map/ppermute | solution.py:24
  61.6 0.7 copy-done.10
  62.3 0.7 copy-done.8
  63.0 0.6 copy-done.9
  63.9 0.7 copy-done.7
  64.6 3.2 fusion.14
  69.4 0.5 convolution_bitcast_fusion.16
  71.9 3.8 collective-permute-start.2
  76.0 1.9 collective-permute-start.4
  77.9 6.2 %collective-permute-start.5 = (bf16[1,4,1,64,256]{4,3,2,1,0:T(8,128)(2,1)S(1)}, bf16[1,4,1,64,256]{4,3,2,1,0:T(8,128)(2,1)S(1)}, u32[]{:S(2)}, u32[]{:S(2)}) collective-permute-start(bf16[1,4,1,64,256]{4,3,2,1,0:T(8,128)(2,1)S(1)} %get-tuple-element.41), channel_id=1, source_target_pairs={{2,0},{4,2},{6,4},{8,6},{10,8},{12,10},{14,12},{16,14},{18,16},{20... | collective-permute-start | bytes 393224 | tf_op jit(solution)/shard_map/ppermute | solution.py:16
  84.1 1.8 fusion.77
  85.9 1.0 convolution_bitcast_fusion.8
  87.0 0.5 convolution_bitcast_fusion.11
  87.9 0.5 convolution_bitcast_fusion.17
  88.5 1.6 pad_maximum_fusion
  90.1 1.0 convolution_bitcast_fusion.9
  91.1 0.8 select_maximum_fusion
  91.9 1.8 fusion.26
  93.7 1.8 fusion.30
  95.5 1.8 fusion.31
  97.3 1.7 fusion.32
  99.8 0.8 copy.41
  100.6 5.8 %all-to-all-start = ((bf16[1,2,8,64,256]{4,3,1,0,2:T(8,128)(2,1)}), bf16[1,2,8,64,256]{4,3,1,0,2:T(8,128)(2,1)}, u32[]{:S(2)}, u32[]{:S(2)}) async-start(bf16[1,2,8,64,256]{4,3,1,0,2:T(8,128)(2,1)} %copy.41), calls=%async_computation | async-start | bytes 1048576 | tf_op jit(solution)/shard_map/all_to_all | solution.py:198
  106.5 2.8 fusion.35
  109.3 2.7 fusion.33
  111.9 2.7 fusion.38
  115.0 6.2 %all-to-all-done = bf16[1,2,8,64,256]{4,3,1,0,2:T(8,128)(2,1)} async-done(((bf16[1,2,8,64,256]{4,3,1,0,2:T(8,128)(2,1)}), bf16[1,2,8,64,256]{4,3,1,0,2:T(8,128)(2,1)}, u32[]{:S(2)}, u32[]{:S(2)}) %all-to-all-start) | async-done | bytes 524320 | tf_op jit(solution)/shard_map/all_to_all | solution.py:198
  121.2 1.4 convolution_bitcast_fusion.4
  122.6 1.4 convolution_bitcast_fusion.5
  124.0 1.4 convolution_bitcast_fusion.6
  125.4 1.2 pad_maximum_fusion.6
  126.7 1.2 copy-done.2
  127.9 7.8 %fusion.11 = (f32[256]{0:T(256)S(1)}, f32[4,8,64]{2,1,0:T(8,128)S(1)}, f32[4,8,64,256]{3,2,1,0:T(8,128)}) fusion(f32[4,8,64]{2,1,0:T(8,128)S(1)} %add_rsqrt_fusion, bf16[1,4,8,64,256]{4,3,2,1,0:T(8,128)(2,1)S(1)} %copy-done.2, pred[4]{0:T(512)(128)(4,1)S(1)} %add_compare_fusion, f32[256]{0:T(256)S(1)} %copy-done.32, f32[4,8,64,256]{3,2,1,0:T(8,128)} %fusion.26, ...), kind=kOutput, calls=%fused_computation.16 | convolution fusion | flops 277346048 | bytes 21252100 | tf_op jit(solution)/shard_map/dot_general | solution.py:29
  135.7 71.9 %psum.31 = f32[256]{0:T(256)S(1)} all-reduce(f32[256]{0:T(256)S(1)} %get-tuple-element.30), channel_id=1, replica_groups=mesh['tm'=8,'height'=16,'cam'=2] {'tm','height','cam'}, use_global_device_ids=true, to_apply=%region_6.7 | all-reduce | flops 256 | bytes 2048 | tf_op jit(solution)/shard_map/psum | solution.py:215
  207.7 0.6 broadcast_multiply_fusion.4
  208.2 2.9 fusion.10
  211.1 1.5 convolution_add_fusion.3
  212.6 1.3 convolution_add_fusion.2
  213.9 2.1 fusion.24
  216.0 174.5 %all-reduce.7.cloned.1.call-done = (f32[3,3,256,256]{3,2,1,0:T(8,128)}, f32[3,256,256]{2,1,0:T(8,128)}, f32[3,256,256]{2,1,0:T(8,128)}) async-done(((f32[3,3,256,256]{3,2,1,0:T(8,128)}, f32[3,256,256]{2,1,0:T(8,128)}, f32[3,256,256]{2,1,0:T(8,128)}), (f32[3,3,256,256]{3,2,1,0:T(8,128)}, f32[3,256,256]{2,1,0:T(8,128)}, f32[3,256,256]{2,1,0:T(8,128)})) %all-reduce.7.cloned.1.call-update) | async-done | bytes 3932176 | tf_op jit(solution)/shard_map/psum | solution.py:215
  390.5 3.4 broadcast_multiply_fusion
  393.9 0.9 broadcast_multiply_fusion.1
  394.8 0.9 broadcast_multiply_fusion.2
  (96 shorter events, 7.9 us)
Async XLA Ops:
  7.2 12.8 %copy-start.3 = (bf16[1,16,1,64,256]{4,3,2,1,0:T(8,128)(2,1)S(1)}, bf16[1,16,1,64,256]{4,3,2,1,0:T(8,128)(2,1)}, u32[]{:S(2)}) copy-start(bf16[1,16,1,64,256]{4,3,2,1,0:T(8,128)(2,1)} %param.13) | copy-start | bytes 1572868
  7.2 12.8 %copy-start.17 = (bf16[3,256,256]{2,1,0:T(8,128)(2,1)S(1)}, bf16[3,256,256]{2,1,0:T(8,128)(2,1)}, u32[]{:S(2)}) copy-start(bf16[3,256,256]{2,1,0:T(8,128)(2,1)} %param.12) | copy-start | bytes 1179652
  11.2 31.1 %copy-start = (bf16[1,4,8,64,256]{4,3,2,1,0:T(8,128)(2,1)}, bf16[1,4,8,64,256]{4,3,2,1,0:T(8,128)(2,1)S(1)}, u32[]{:S(2)}) copy-start(bf16[1,4,8,64,256]{4,3,2,1,0:T(8,128)(2,1)S(1)} %fusion.5) | copy-start | bytes 3145732
  12.0 24.0 %collective-permute-start = (bf16[1,4,1,64,256]{4,3,2,1,0:T(8,128)(2,1)}, bf16[1,4,1,64,256]{4,3,2,1,0:T(8,128)(2,1)S(1)}, u32[]{:S(2)}, u32[]{:S(2)}) collective-permute-start(bf16[1,4,1,64,256]{4,3,2,1,0:T(8,128)(2,1)} %get-tuple-element.42), channel_id=1, source_target_pairs={{0,2},{2,4},{4,6},{6,8},{8,10},{10,12},{12,14},{14,16},{16,18},{18... | collective-permute-start | bytes 393224 | tf_op jit(solution)/shard_map/ppermute | solution.py:15
  15.5 20.6 %collective-permute-start.1 = (bf16[1,4,1,64,256]{4,3,2,1,0:T(8,128)(2,1)}, bf16[1,4,1,64,256]{4,3,2,1,0:T(8,128)(2,1)S(1)}, u32[]{:S(2)}, u32[]{:S(2)}) collective-permute-start(bf16[1,4,1,64,256]{4,3,2,1,0:T(8,128)(2,1)} %get-tuple-element.43), channel_id=1, source_target_pairs={{2,0},{4,2},{6,4},{8,6},{10,8},{12,10},{14,12},{16,14},{18,16},{20... | collective-permute-start | bytes 393224 | tf_op jit(solution)/shard_map/ppermute | solution.py:16
  20.7 9.6 %copy-start.14 = (bf16[3,3,256,256]{3,2,1,0:T(8,128)(2,1)S(1)}, bf16[3,3,256,256]{3,2,1,0:T(8,128)(2,1)}, u32[]{:S(2)}) copy-start(bf16[3,3,256,256]{3,2,1,0:T(8,128)(2,1)} %param.10) | copy-start | bytes 3538948
  21.8 27.7 %all-to-all-start.1 = ((bf16[1,16,1,64,256]{4,3,2,0,1:T(8,128)(2,1)}), bf16[1,16,1,64,256]{4,3,2,0,1:T(8,128)(2,1)S(1)}, u32[]{:S(2)}, u32[]{:S(2)}) async-start(bf16[1,16,1,64,256]{4,3,2,0,1:T(8,128)(2,1)} %fusion.23), calls=%async_computation.1 | async-start | bytes 1048576 | tf_op jit(solution)/shard_map/all_to_all | solution.py:201
  33.6 3.3 copy-start.15
  36.1 6.2 %copy-start.29 = (bf16[1,4,1,64,256]{4,3,2,1,0:T(8,128)(2,1)}, bf16[1,4,1,64,256]{4,3,2,1,0:T(8,128)(2,1)S(1)}, u32[]{:S(2)}) copy-start(bf16[1,4,1,64,256]{4,3,2,1,0:T(8,128)(2,1)S(1)} %collective-permute-done) | copy-start | bytes 393220
  36.1 2.6 copy-start.27
  47.7 5.2 %copy-start.19 = (bf16[3,256,256]{2,1,0:T(8,128)(2,1)S(1)}, bf16[3,256,256]{2,1,0:T(8,128)(2,1)}, u32[]{:S(2)}) copy-start(bf16[3,256,256]{2,1,0:T(8,128)(2,1)} %param.11) | copy-start | bytes 1179652
  49.5 0.8 copy-start.5
  50.3 2.6 copy-start.6
  50.3 11.2 %copy-start.13 = (f32[4,8,64,256]{3,2,1,0:T(8,128)S(1)}, f32[4,8,64,256]{3,2,1,0:T(8,128)}, u32[]{:S(2)}) copy-start(f32[4,8,64,256]{3,2,1,0:T(8,128)} %fusion.49) | copy-start | bytes 6291460
  51.6 9.1 %collective-permute-start.3 = (bf16[1,1,8,64,256]{4,3,2,1,0:T(8,128)(2,1)S(1)}, bf16[1,1,8,64,256]{4,3,2,1,0:T(8,128)(2,1)S(1)}, u32[]{:S(2)}, u32[]{:S(2)}) collective-permute-start(bf16[1,1,8,64,256]{4,3,2,1,0:T(8,128)(2,1)S(1)} %get-tuple-element.47), channel_id=1, source_target_pairs={{32,0},{64,32},{96,64},{128,96},{160,128},{192,160},{224,192},{33,... | collective-permute-start | bytes 786440 | tf_op jit(solution)/shard_map/ppermute | solution.py:24
  52.9 8.7 %copy-start.12 = (f32[4,8,64,256]{3,2,1,0:T(8,128)S(1)}, f32[4,8,64,256]{3,2,1,0:T(8,128)}, u32[]{:S(2)}) copy-start(f32[4,8,64,256]{3,2,1,0:T(8,128)} %fusion.48) | copy-start | bytes 6291460
  53.3 8.3 %copy-start.11 = (f32[4,8,64,256]{3,2,1,0:T(8,128)S(1)}, f32[4,8,64,256]{3,2,1,0:T(8,128)}, u32[]{:S(2)}) copy-start(f32[4,8,64,256]{3,2,1,0:T(8,128)} %fusion.47) | copy-start | bytes 6291460
  60.7 1.6 copy-start.10
  61.0 2.0 copy-start.8
  61.1 2.6 copy-start.9
  61.3 2.6 copy-start.1
  61.3 3.3 copy-start.7
  61.3 3.3 copy-start.28
  71.3 4.3 %copy-start.20 = (bf16[3,256,256]{2,1,0:T(8,128)(2,1)S(1)}, bf16[3,256,256]{2,1,0:T(8,128)(2,1)}, u32[]{:S(2)}) copy-start(bf16[3,256,256]{2,1,0:T(8,128)(2,1)} %param.11) | copy-start | bytes 1179652
  71.8 12.3 %copy-start.16 = (bf16[3,3,256,256]{3,2,1,0:T(8,128)(2,1)S(1)}, bf16[3,3,256,256]{3,2,1,0:T(8,128)(2,1)}, u32[]{:S(2)}) copy-start(bf16[3,3,256,256]{3,2,1,0:T(8,128)(2,1)} %reverse_bitcast_fusion) | copy-start | bytes 3538948
  71.9 27.2 %collective-permute-start.2 = (bf16[1,1,8,64,256]{4,3,2,1,0:T(8,128)(2,1)S(1)}, bf16[1,1,8,64,256]{4,3,2,1,0:T(8,128)(2,1)S(1)}, u32[]{:S(2)}, u32[]{:S(2)}) collective-permute-start(bf16[1,1,8,64,256]{4,3,2,1,0:T(8,128)(2,1)S(1)} %slice.255), channel_id=1, source_target_pairs={{0,32},{32,64},{64,96},{96,128},{128,160},{160,192},{192,224},{1,3... | collective-permute-start | bytes 786440 | tf_op jit(solution)/shard_map/ppermute | solution.py:24
  76.0 15.1 %collective-permute-start.4 = (bf16[1,4,1,64,256]{4,3,2,1,0:T(8,128)(2,1)S(1)}, bf16[1,4,1,64,256]{4,3,2,1,0:T(8,128)(2,1)S(1)}, u32[]{:S(2)}, u32[]{:S(2)}) collective-permute-start(bf16[1,4,1,64,256]{4,3,2,1,0:T(8,128)(2,1)S(1)} %get-tuple-element.40), channel_id=1, source_target_pairs={{0,2},{2,4},{4,6},{6,8},{8,10},{10,12},{12,14},{14,16},{16,18},{18... | collective-permute-start | bytes 393224 | tf_op jit(solution)/shard_map/ppermute | solution.py:15
  77.9 13.2 %collective-permute-start.5 = (bf16[1,4,1,64,256]{4,3,2,1,0:T(8,128)(2,1)S(1)}, bf16[1,4,1,64,256]{4,3,2,1,0:T(8,128)(2,1)S(1)}, u32[]{:S(2)}, u32[]{:S(2)}) collective-permute-start(bf16[1,4,1,64,256]{4,3,2,1,0:T(8,128)(2,1)S(1)} %get-tuple-element.41), channel_id=1, source_target_pairs={{2,0},{4,2},{6,4},{8,6},{10,8},{12,10},{14,12},{16,14},{18,16},{20... | collective-permute-start | bytes 393224 | tf_op jit(solution)/shard_map/ppermute | solution.py:16
  87.0 0.9 copy-start.30
  91.1 2.6 copy-start.31
  99.1 0.7 copy-start.23
  100.6 20.6 %all-to-all-start = ((bf16[1,2,8,64,256]{4,3,1,0,2:T(8,128)(2,1)}), bf16[1,2,8,64,256]{4,3,1,0,2:T(8,128)(2,1)}, u32[]{:S(2)}, u32[]{:S(2)}) async-start(bf16[1,2,8,64,256]{4,3,1,0,2:T(8,128)(2,1)} %copy.41), calls=%async_computation | async-start | bytes 1048576 | tf_op jit(solution)/shard_map/all_to_all | solution.py:198
  106.4 284.1 %all-reduce.7.cloned.1.call-start = ((), (), s32[]{:S(2)}) async-start(), calls=%async_computation.2 | async-start | bytes 7864320 | tf_op jit(solution)/shard_map/psum | solution.py:215
  111.9 2.7 copy-start.24
  114.6 6.6 %copy-start.4 = (bf16[1,16,1,64,256]{4,3,2,1,0:T(8,128)(2,1)S(1)}, bf16[1,16,1,64,256]{4,3,2,1,0:T(8,128)(2,1)}, u32[]{:S(2)}) copy-start(bf16[1,16,1,64,256]{4,3,2,1,0:T(8,128)(2,1)} %param.13) | copy-start | bytes 1572868
  122.5 2.8 copy-start.21
  122.6 2.8 copy-start.22
  126.7 1.2 copy-start.2
  126.7 1.2 copy-start.32
  208.2 2.9 copy-start.18
  390.5 3.4 copy-start.26
  390.5 4.3 %copy-start.25 = (f32[3,256,256]{2,1,0:T(8,128)S(1)}, f32[3,256,256]{2,1,0:T(8,128)}, u32[]{:S(2)}) copy-start(f32[3,256,256]{2,1,0:T(8,128)} %get-tuple-element.33) | copy-start | bytes 2359300
Sparse Core Ops, SparseCore 0:
  126.8 263.6 all-reduce.6
where the time goes:
time: 404 us; the launch traced here: 403 us
  waiting for transfers between devices  188 us (47%)
  blocking collectives  71.9 us (18%)
  matrix products  62.2 us (15%)
  starting transfers between devices  35.4 us (9%)
  other arithmetic  16.8 us (4%)
  between operations  15.3 us (4%)
  local copies, waits for them, and re-layouts  13.2 us (3%)
    psum x1, waiting for transfers between devices, on_device(): lax.psum((mix_gradient, temporal_gradient, spatial_gradient, gain_gradien...  174 us
    psum x1, blocking collectives, on_device(): lax.psum((mix_gradient, temporal_gradient, spatial_gradient, gain_gradien...  71.9 us
    dot_general x24, matrix products, project(): product = jnp.dot(flat_rows, weight, preferred_element_type=jnp.float32)  48.4 us
    dot_general x15, matrix products, outer_sum(): lax.dot_general(left_rows.reshape(-1, left_rows.shape[-1]), right_rows.re...  10.9 us
    ppermute x2, starting transfers between devices, extended(): after = lax.ppermute(initial, axis, down)  10.7 us
    all_to_all x1, starting transfers between devices, on_device(): lax.all_to_all(regrouped_gradient, 'tm', split_axis=1, concat_axis=2, til...  8.46 us
  transfers between devices with their start and end apart: 9, of which 3 were waited for; matrix products, arithmetic and copies ran while one was open for 15% of the time, Pallas kernels for 0%

commit v1 on v0

--- a/solution.py
+++ b/solution.py
@@ -213,7 +213,10 @@
         normed_gradient, unit_rows, inverse, norm_gain, present
     )
     mix_gradient, temporal_gradient, spatial_gradient, gain_gradient = lax.psum(
-        (mix_gradient, temporal_gradient, spatial_gradient, gain_gradient), ("tm", "height", "cam")
+        lax.psum(
+            (mix_gradient, temporal_gradient, spatial_gradient, gain_gradient), ("height", "cam")
+        ),
+        "tm",
     )
     cell_count = (
         video_clip.shape[0]

time: 404 us -> 343 us (0.85)
  waiting for transfers between devices: 188 us -> 130 us
  matrix products: 62.2 us -> 49.5 us
    psum x1, waiting for transfers between devices: 174 us -> 96.4 us  [on_device(): lax.psum((mix_gradient, temporal_gradient, spatial_gradient, gain_gradien...]
    psum x0 -> x1, waiting for transfers between devices: none -> 20.8 us  [on_device(): lax.psum(lax.psum((mix_gradient, temporal_gradient, spatial_gradient, gai...]
    psum x0 -> x1, blocking collectives: none -> 18.1 us  [on_device(): lax.psum(lax.psum((mix_gradient, temporal_gradient, spatial_gradient, gai...]
    dot_general x24, matrix products: 48.4 us -> 31.4 us  [project(): product = jnp.dot(flat_rows, weight, preferred_element_type=jnp.float32)]
    psum x1, blocking collectives: 71.9 us -> 55.3 us  [on_device(): lax.psum((mix_gradient, temporal_gradient, spatial_gradient, gain_gradien...]
    unnamed x67 -> x77, local copies, waits for them, and re-layouts: 7.41 us -> 9.69 us
  transfers between devices with their start and end apart: 9 -> 10, of which waited for: 3 -> 6; matrix products, arithmetic and copies ran while one was open for 15% -> 15% of each run, Pallas kernels for 0% -> 0%
where the time goes in v1:
time: 343 us; the launch traced here: 341 us
  waiting for transfers between devices  130 us (38%)
  blocking collectives  73.3 us (21%)
  matrix products  49.5 us (14%)
  starting transfers between devices  38 us (11%)
  other arithmetic  20.1 us (6%)
  between operations  15.3 us (4%)
  local copies, waits for them, and re-layouts  14.6 us (4%)
    psum x1, waiting for transfers between devices, on_device(): lax.psum((mix_gradient, temporal_gradient, spatial_gradient, gain_gradien...  96.4 us
    psum x1, blocking collectives, on_device(): lax.psum((mix_gradient, temporal_gradient, spatial_gradient, gain_gradien...  55.3 us
    dot_general x24, matrix products, project(): product = jnp.dot(flat_rows, weight, preferred_element_type=jnp.float32)  31.4 us
    psum x1, waiting for transfers between devices, on_device(): lax.psum(lax.psum((mix_gradient, temporal_gradient, spatial_gradient, gai...  20.8 us
    psum x1, blocking collectives, on_device(): lax.psum(lax.psum((mix_gradient, temporal_gradient, spatial_gradient, gai...  18.1 us
    dot_general x15, matrix products, outer_sum(): lax.dot_general(left_rows.reshape(-1, left_rows.shape[-1]), right_rows.re...  12.9 us
    ppermute x2, starting transfers between devices, extended(): after = lax.ppermute(initial, axis, down)  10.5 us
    unnamed x77, local copies, waits for them, and re-layouts  9.69 us
  transfers between devices with their start and end apart: 10, of which 6 were waited for; matrix products, arithmetic and copies ran while one was open for 15% of the time, Pallas kernels for 0%

profile of v1, /device:TPU:2, one launch (start us, length us, event | category | flops | bytes accessed | tf_op | source)
XLA Modules:
  0.0 341.1 jit_solution(17884851703520734297)
XLA Ops:
  7.9 1.6 fusion.12
  9.6 1.6 fusion.5
  11.3 3.5 %collective-permute-start = (bf16[1,4,1,64,256]{4,3,2,1,0:T(8,128)(2,1)S(1)}, bf16[1,4,1,64,256]{4,3,2,1,0:T(8,128)(2,1)S(1)}, u32[]{:S(2)}, u32[]{:S(2)}) collective-permute-start(bf16[1,4,1,64,256]{4,3,2,1,0:T(8,128)(2,1)S(1)} %get-tuple-element.45), channel_id=1, source_target_pairs={{0,2},{2,4},{4,6},{6,8},{8,10},{10,12},{12,14},{14,16},{16,18},{18... | collective-permute-start | bytes 393224 | tf_op jit(solution)/shard_map/ppermute | solution.py:15
  14.8 4.5 %collective-permute-start.1 = (bf16[1,4,1,64,256]{4,3,2,1,0:T(8,128)(2,1)S(1)}, bf16[1,4,1,64,256]{4,3,2,1,0:T(8,128)(2,1)}, u32[]{:S(2)}, u32[]{:S(2)}) collective-permute-start(bf16[1,4,1,64,256]{4,3,2,1,0:T(8,128)(2,1)S(1)} %get-tuple-element.46), channel_id=1, source_target_pairs={{2,0},{4,2},{6,4},{8,6},{10,8},{12,10},{14,12},{16,14},{18,16},{20... | collective-permute-start | bytes 393224 | tf_op jit(solution)/shard_map/ppermute | solution.py:16
  19.9 1.2 fusion.23
  21.1 8.5 %all-to-all-start.1 = ((bf16[1,16,1,64,256]{4,3,2,0,1:T(8,128)(2,1)}), bf16[1,16,1,64,256]{4,3,2,0,1:T(8,128)(2,1)}, u32[]{:S(2)}, u32[]{:S(2)}) async-start(bf16[1,16,1,64,256]{4,3,2,0,1:T(8,128)(2,1)} %fusion.23), calls=%async_computation.1 | async-start | bytes 1048576 | tf_op jit(solution)/shard_map/all_to_all | solution.py:201
  29.5 2.7 fusion.42
  32.2 0.7 copy-done.33
  32.9 1.8 select_maximum_fusion.2
  34.7 1.8 fusion.44
  36.5 1.8 fusion.45
  38.3 1.8 fusion.46
  40.0 1.8 fusion.51
  41.9 1.8 fusion.47
  43.7 1.7 fusion.48
  45.5 1.8 fusion.49
  47.2 1.2 copy.91
  48.5 1.3 collective-permute-start.3
  49.8 1.5 convolution_bitcast_fusion
  51.4 1.5 fusion.66
  52.9 4.7 %collective-permute-done.3 = bf16[1,1,8,64,256]{4,3,2,1,0:T(8,128)(2,1)S(1)} collective-permute-done((bf16[1,1,8,64,256]{4,3,2,1,0:T(8,128)(2,1)S(1)}, bf16[1,1,8,64,256]{4,3,2,1,0:T(8,128)(2,1)S(1)}, u32[]{:S(2)}, u32[]{:S(2)}) %collective-permute-start.3) | collective-permute-done | bytes 262176 | tf_op jit(solution)/shard_map/ppermute | solution.py:24
  58.5 0.7 copy-done.12
  59.2 0.7 copy-done.10
  59.9 0.6 copy-done.11
  60.9 0.7 copy-done.9
  61.5 3.5 %fusion.14 = (bf16[4,8,64,256]{3,2,1,0:T(8,128)(2,1)S(1)}, bf16[4,8,64,256]{3,2,1,0:T(8,128)(2,1)S(1)}) fusion(f32[1,2,2,8,64,256]{5,4,3,2,1,0:T(8,128)S(1)} %copy.46, f32[4,8,64,256]{3,2,1,0:T(8,128)S(1)} %copy-done.15, bf16[3,3,256,256]{3,2,1,0:T(8,128)(2,1)} %param.10, bf16[1,4,1,64,256]{4,3,2,1,0:T(8,128)(2,1)} %collective-permute-done.1, ...), kind=kOutput, calls=%fused_computation.21 | convolution fusion | flops 278921216 | bytes 22282240 | tf_op jit(solution)/shard_map/dot_general | solution.py:29
  65.1 1.1 fusion.137
  68.9 1.2 convolution_bitcast_fusion.10
  70.1 1.2 convolution_bitcast_fusion.12
  71.3 4.0 %collective-permute-start.2 = (bf16[1,1,8,64,256]{4,3,2,1,0:T(8,128)(2,1)S(1)}, bf16[1,1,8,64,256]{4,3,2,1,0:T(8,128)(2,1)S(1)}, u32[]{:S(2)}, u32[]{:S(2)}) collective-permute-start(bf16[1,1,8,64,256]{4,3,2,1,0:T(8,128)(2,1)S(1)} %slice.255), channel_id=1, source_target_pairs={{0,32},{32,64},{64,96},{96,128},{128,160},{160,192},{192,224},{1,3... | collective-permute-start | bytes 786440 | tf_op jit(solution)/shard_map/ppermute | solution.py:24
  76.1 1.2 maximum_bitcast_fusion
  77.4 2.1 convolution_bitcast_fusion.11
  80.2 0.8 copy.41
  81.1 8.3 %all-to-all-start = ((bf16[1,2,8,64,256]{4,3,1,0,2:T(8,128)(2,1)}), bf16[1,2,8,64,256]{4,3,1,0,2:T(8,128)(2,1)S(1)}, u32[]{:S(2)}, u32[]{:S(2)}) async-start(bf16[1,2,8,64,256]{4,3,1,0,2:T(8,128)(2,1)} %copy.41), calls=%async_computation | async-start | bytes 1048576 | tf_op jit(solution)/shard_map/all_to_all | solution.py:198
  89.5 1.3 maximum_bitcast_fusion.2
  90.8 2.1 convolution_bitcast_fusion.8
  92.8 2.1 convolution_bitcast_fusion.9
  94.9 1.6 pad_maximum_fusion
  96.9 6.9 %all-to-all-done = bf16[1,2,8,64,256]{4,3,1,0,2:T(8,128)(2,1)S(1)} async-done(((bf16[1,2,8,64,256]{4,3,1,0,2:T(8,128)(2,1)}), bf16[1,2,8,64,256]{4,3,1,0,2:T(8,128)(2,1)S(1)}, u32[]{:S(2)}, u32[]{:S(2)}) %all-to-all-start) | async-done | bytes 524320 | tf_op jit(solution)/shard_map/all_to_all | solution.py:198
  105.1 1.2 pad_maximum_fusion.6
  106.4 1.2 copy-done.17
  107.6 1.6 copy.47
  109.2 1.3 reverse_bitcast_fusion
  110.6 1.9 collective-permute-start.4
  112.5 6.0 %collective-permute-start.5 = (bf16[1,4,1,64,256]{4,3,2,1,0:T(8,128)(2,1)S(1)}, bf16[1,4,1,64,256]{4,3,2,1,0:T(8,128)(2,1)S(1)}, u32[]{:S(2)}, u32[]{:S(2)}) collective-permute-start(bf16[1,4,1,64,256]{4,3,2,1,0:T(8,128)(2,1)S(1)} %get-tuple-element.44), channel_id=1, source_target_pairs={{2,0},{4,2},{6,4},{8,6},{10,8},{12,10},{14,12},{16,14},{18,16},{20... | collective-permute-start | bytes 393224 | tf_op jit(solution)/shard_map/ppermute | solution.py:16
  118.6 1.8 fusion.77
  120.8 0.9 collective-permute-done.5
  121.7 0.7 copy-done.31
  122.4 0.8 select_maximum_fusion
  123.2 1.9 fusion.26
  125.1 96.4 %all-reduce.9.cloned.1.call-done = (f32[3,3,256,256]{3,2,1,0:T(8,128)}, f32[3,256,256]{2,1,0:T(8,128)}, f32[3,256,256]{2,1,0:T(8,128)}) async-done(((f32[3,3,256,256]{3,2,1,0:T(8,128)}, f32[3,256,256]{2,1,0:T(8,128)}, f32[3,256,256]{2,1,0:T(8,128)}), (f32[3,3,256,256]{3,2,1,0:T(8,128)}, f32[3,256,256]{2,1,0:T(8,128)}, f32[3,256,256]{2,1,0:T(8,128)})) %all-reduce.9.cloned.1.call-update) | async-done | bytes 3932176 | tf_op jit(solution)/shard_map/psum | solution.py:216
  221.5 1.5 fusion.35
  225.3 0.7 copy-done.7
  226.3 0.7 copy-done.6
  227.0 2.7 fusion.11
  229.7 55.3 %psum.62 = f32[256]{0:T(256)S(1)} all-reduce(f32[256]{0:T(256)S(1)} %get-tuple-element.30), channel_id=1, replica_groups=mesh['tm'=8,'height'=16,'cam'=2] {'height','cam'}, use_global_device_ids=true, to_apply=%region_9.10 | all-reduce | flops 256 | bytes 2048 | tf_op jit(solution)/shard_map/psum | solution.py:216
  285.0 18.1 %psum.63 = f32[256]{0:T(256)S(1)} all-reduce(f32[256]{0:T(256)S(1)} %psum.62), channel_id=1, replica_groups=mesh['tm'=8,'height'=16,'cam'=2] {'tm'}, use_global_device_ids=true, to_apply=%region_10.11 | all-reduce | flops 256 | bytes 2048 | tf_op jit(solution)/shard_map/psum | solution.py:215
  303.1 0.6 broadcast_multiply_fusion.4
  303.6 2.8 fusion.10
  307.0 1.1 fusion.24
  308.1 20.8 %all-reduce.11.cloned.1.call-done = (f32[3,3,256,256]{3,2,1,0:T(8,128)}, f32[3,256,256]{2,1,0:T(8,128)}, f32[3,256,256]{2,1,0:T(8,128)}) async-done(((f32[3,3,256,256]{3,2,1,0:T(8,128)}, f32[3,256,256]{2,1,0:T(8,128)}, f32[3,256,256]{2,1,0:T(8,128)}), (f32[3,3,256,256]{3,2,1,0:T(8,128)}, f32[3,256,256]{2,1,0:T(8,128)}, f32[3,256,256]{2,1,0:T(8,128)})) %all-reduce.11.cloned.1.call-update) | async-done | bytes 3932176 | tf_op jit(solution)/shard_map/psum | solution.py:215
  329.0 3.4 broadcast_multiply_fusion
  332.4 0.9 broadcast_multiply_fusion.1
  333.3 0.9 broadcast_multiply_fusion.2
  (110 shorter events, 11.7 us)
Async XLA Ops:
  7.2 12.1 %copy-start.8 = (bf16[1,16,1,64,256]{4,3,2,1,0:T(8,128)(2,1)S(1)}, bf16[1,16,1,64,256]{4,3,2,1,0:T(8,128)(2,1)}, u32[]{:S(2)}) copy-start(bf16[1,16,1,64,256]{4,3,2,1,0:T(8,128)(2,1)} %param.13) | copy-start | bytes 1572868
  7.2 12.1 %copy-start.22 = (bf16[3,256,256]{2,1,0:T(8,128)(2,1)S(1)}, bf16[3,256,256]{2,1,0:T(8,128)(2,1)}, u32[]{:S(2)}) copy-start(bf16[3,256,256]{2,1,0:T(8,128)(2,1)} %param.12) | copy-start | bytes 1179652
  11.2 28.8 %copy-start = (bf16[1,4,8,64,256]{4,3,2,1,0:T(8,128)(2,1)}, bf16[1,4,8,64,256]{4,3,2,1,0:T(8,128)(2,1)S(1)}, u32[]{:S(2)}) copy-start(bf16[1,4,8,64,256]{4,3,2,1,0:T(8,128)(2,1)S(1)} %fusion.5) | copy-start | bytes 3145732
  11.3 21.0 %collective-permute-start = (bf16[1,4,1,64,256]{4,3,2,1,0:T(8,128)(2,1)S(1)}, bf16[1,4,1,64,256]{4,3,2,1,0:T(8,128)(2,1)S(1)}, u32[]{:S(2)}, u32[]{:S(2)}) collective-permute-start(bf16[1,4,1,64,256]{4,3,2,1,0:T(8,128)(2,1)S(1)} %get-tuple-element.45), channel_id=1, source_target_pairs={{0,2},{2,4},{4,6},{6,8},{8,10},{10,12},{12,14},{14,16},{16,18},{18... | collective-permute-start | bytes 393224 | tf_op jit(solution)/shard_map/ppermute | solution.py:15
  14.8 18.1 %collective-permute-start.1 = (bf16[1,4,1,64,256]{4,3,2,1,0:T(8,128)(2,1)S(1)}, bf16[1,4,1,64,256]{4,3,2,1,0:T(8,128)(2,1)}, u32[]{:S(2)}, u32[]{:S(2)}) collective-permute-start(bf16[1,4,1,64,256]{4,3,2,1,0:T(8,128)(2,1)S(1)} %get-tuple-element.46), channel_id=1, source_target_pairs={{2,0},{4,2},{6,4},{8,6},{10,8},{12,10},{14,12},{16,14},{18,16},{20... | collective-permute-start | bytes 393224 | tf_op jit(solution)/shard_map/ppermute | solution.py:16
  21.1 26.2 %all-to-all-start.1 = ((bf16[1,16,1,64,256]{4,3,2,0,1:T(8,128)(2,1)}), bf16[1,16,1,64,256]{4,3,2,0,1:T(8,128)(2,1)}, u32[]{:S(2)}, u32[]{:S(2)}) async-start(bf16[1,16,1,64,256]{4,3,2,0,1:T(8,128)(2,1)} %fusion.23), calls=%async_computation.1 | async-start | bytes 1048576 | tf_op jit(solution)/shard_map/all_to_all | solution.py:201
  32.2 2.4 copy-start.16
  32.2 0.7 copy-start.33
  38.3 1.8 copy-start.34
  45.5 4.4 %copy-start.23 = (bf16[3,256,256]{2,1,0:T(8,128)(2,1)S(1)}, bf16[3,256,256]{2,1,0:T(8,128)(2,1)}, u32[]{:S(2)}) copy-start(bf16[3,256,256]{2,1,0:T(8,128)(2,1)} %param.11) | copy-start | bytes 1179652
  47.2 11.3 %copy-start.15 = (f32[4,8,64,256]{3,2,1,0:T(8,128)S(1)}, f32[4,8,64,256]{3,2,1,0:T(8,128)}, u32[]{:S(2)}) copy-start(f32[4,8,64,256]{3,2,1,0:T(8,128)} %fusion.49) | copy-start | bytes 6291460
  48.5 4.4 %copy-start.4 = (bf16[1,8,2,1,64,256]{5,4,1,2,3,0:T(8,128)(2,1)}, bf16[1,8,2,1,64,256]{5,4,1,2,3,0:T(8,128)(2,1)S(1)}, u32[]{:S(2)}) copy-start(bf16[1,8,2,1,64,256]{5,4,1,2,3,0:T(8,128)(2,1)S(1)} %copy.91) | copy-start | bytes 1572868
  48.5 9.1 %collective-permute-start.3 = (bf16[1,1,8,64,256]{4,3,2,1,0:T(8,128)(2,1)S(1)}, bf16[1,1,8,64,256]{4,3,2,1,0:T(8,128)(2,1)S(1)}, u32[]{:S(2)}, u32[]{:S(2)}) collective-permute-start(bf16[1,1,8,64,256]{4,3,2,1,0:T(8,128)(2,1)S(1)} %get-tuple-element.50), channel_id=1, source_target_pairs={{32,0},{64,32},{96,64},{128,96},{160,128},{192,160},{224,192},{33,... | collective-permute-start | bytes 786440 | tf_op jit(solution)/shard_map/ppermute | solution.py:24
  49.8 8.7 %copy-start.14 = (f32[4,8,64,256]{3,2,1,0:T(8,128)S(1)}, f32[4,8,64,256]{3,2,1,0:T(8,128)}, u32[]{:S(2)}) copy-start(f32[4,8,64,256]{3,2,1,0:T(8,128)} %fusion.48) | copy-start | bytes 6291460
  51.4 7.2 %copy-start.13 = (f32[4,8,64,256]{3,2,1,0:T(8,128)S(1)}, f32[4,8,64,256]{3,2,1,0:T(8,128)}, u32[]{:S(2)}) copy-start(f32[4,8,64,256]{3,2,1,0:T(8,128)} %fusion.47) | copy-start | bytes 6291460
  57.6 1.6 copy-start.12
  58.0 1.9 copy-start.10
  58.0 2.6 copy-start.11
  58.2 2.6 copy-start.1
  58.2 3.3 copy-start.9
  65.1 1.2 copy-start.24
  71.3 4.3 %copy-start.35 = (bf16[1,4,1,64,256]{4,3,2,1,0:T(8,128)(2,1)S(1)}, bf16[1,4,1,64,256]{4,3,2,1,0:T(8,128)(2,1)}, u32[]{:S(2)}) copy-start(bf16[1,4,1,64,256]{4,3,2,1,0:T(8,128)(2,1)} %copy-done.33) | copy-start | bytes 393220
  71.3 8.2 %collective-permute-start.2 = (bf16[1,1,8,64,256]{4,3,2,1,0:T(8,128)(2,1)S(1)}, bf16[1,1,8,64,256]{4,3,2,1,0:T(8,128)(2,1)S(1)}, u32[]{:S(2)}, u32[]{:S(2)}) collective-permute-start(bf16[1,1,8,64,256]{4,3,2,1,0:T(8,128)(2,1)S(1)} %slice.255), channel_id=1, source_target_pairs={{0,32},{32,64},{64,96},{96,128},{128,160},{160,192},{192,224},{1,3... | collective-permute-start | bytes 786440 | tf_op jit(solution)/shard_map/ppermute | solution.py:24
  79.5 0.7 copy-start.27
  80.2 10.5 %copy-start.5 = (bf16[1,8,2,1,64,256]{5,4,1,2,3,0:T(8,128)(2,1)S(1)}, bf16[1,8,2,1,64,256]{5,4,1,2,3,0:T(8,128)(2,1)}, u32[]{:S(2)}) copy-start(bf16[1,8,2,1,64,256]{5,4,1,2,3,0:T(8,128)(2,1)} %copy-done.4) | copy-start | bytes 1572868
  81.1 22.7 %all-to-all-start = ((bf16[1,2,8,64,256]{4,3,1,0,2:T(8,128)(2,1)}), bf16[1,2,8,64,256]{4,3,1,0,2:T(8,128)(2,1)S(1)}, u32[]{:S(2)}, u32[]{:S(2)}) async-start(bf16[1,2,8,64,256]{4,3,1,0,2:T(8,128)(2,1)} %copy.41), calls=%async_computation | async-start | bytes 1048576 | tf_op jit(solution)/shard_map/all_to_all | solution.py:198
  89.4 132.1 %all-reduce.9.cloned.1.call-start = ((), (), s32[]{:S(2)}) async-start(), calls=%async_computation.2 | async-start | bytes 7864320 | tf_op jit(solution)/shard_map/psum | solution.py:216
  89.4 5.5 %copy-start.20 = (f32[1,3,256,256]{3,2,1,0:T(8,128)S(1)}, f32[1,3,256,256]{3,2,1,0:T(8,128)}, u32[]{:S(2)}) copy-start(f32[1,3,256,256]{3,2,1,0:T(8,128)} %get-tuple-element.52) | copy-start | bytes 2359300
  89.5 5.5 %copy-start.21 = (f32[1,3,256,256]{3,2,1,0:T(8,128)S(1)}, f32[1,3,256,256]{3,2,1,0:T(8,128)}, u32[]{:S(2)}) copy-start(f32[1,3,256,256]{3,2,1,0:T(8,128)} %get-tuple-element.53) | copy-start | bytes 2359300
  94.9 1.6 copy-start.28
  104.1 1.0 copy-start.25
  104.1 1.0 copy-start.26
  106.4 1.3 copy-start.17
  106.4 222.6 %all-reduce.11.cloned.1.call-start = ((), (), s32[]{:S(2)}) async-start(), calls=%async_computation.3 | async-start | bytes 7864320 | tf_op jit(solution)/shard_map/psum | solution.py:215
  110.5 12.6 %copy-start.18 = (bf16[3,3,256,256]{3,2,1,0:T(8,128)(2,1)}, bf16[3,3,256,256]{3,2,1,0:T(8,128)(2,1)S(1)}, u32[]{:S(2)}) copy-start(bf16[3,3,256,256]{3,2,1,0:T(8,128)(2,1)S(1)} %reverse_bitcast_fusion) | copy-start | bytes 3538948
  110.6 10.3 %collective-permute-start.4 = (bf16[1,4,1,64,256]{4,3,2,1,0:T(8,128)(2,1)S(1)}, bf16[1,4,1,64,256]{4,3,2,1,0:T(8,128)(2,1)S(1)}, u32[]{:S(2)}, u32[]{:S(2)}) collective-permute-start(bf16[1,4,1,64,256]{4,3,2,1,0:T(8,128)(2,1)S(1)} %get-tuple-element.43), channel_id=1, source_target_pairs={{0,2},{2,4},{4,6},{6,8},{8,10},{10,12},{12,14},{14,16},{16,18},{18... | collective-permute-start | bytes 393224 | tf_op jit(solution)/shard_map/ppermute | solution.py:15
  112.5 9.2 %collective-permute-start.5 = (bf16[1,4,1,64,256]{4,3,2,1,0:T(8,128)(2,1)S(1)}, bf16[1,4,1,64,256]{4,3,2,1,0:T(8,128)(2,1)S(1)}, u32[]{:S(2)}, u32[]{:S(2)}) collective-permute-start(bf16[1,4,1,64,256]{4,3,2,1,0:T(8,128)(2,1)S(1)} %get-tuple-element.44), channel_id=1, source_target_pairs={{2,0},{4,2},{6,4},{8,6},{10,8},{12,10},{14,12},{16,14},{18,16},{20... | collective-permute-start | bytes 393224 | tf_op jit(solution)/shard_map/ppermute | solution.py:16
  120.8 2.3 copy-start.36
  121.7 0.7 copy-start.31
  221.5 1.5 copy-start.19
  224.3 1.6 copy-start.7
  224.4 1.6 copy-start.37
  224.8 1.5 copy-start.2
  224.8 2.2 copy-start.6
  224.8 2.2 copy-start.32
  227.0 76.6 %copy-start.3 = (bf16[1,4,8,64,256]{4,3,2,1,0:T(8,128)(2,1)S(1)}, bf16[1,4,8,64,256]{4,3,2,1,0:T(8,128)(2,1)}, u32[]{:S(2)}) copy-start(bf16[1,4,8,64,256]{4,3,2,1,0:T(8,128)(2,1)} %param.7) | copy-start | bytes 3145732
  329.0 3.4 copy-start.30
  329.0 4.3 %copy-start.29 = (f32[3,256,256]{2,1,0:T(8,128)S(1)}, f32[3,256,256]{2,1,0:T(8,128)}, u32[]{:S(2)}) copy-start(f32[3,256,256]{2,1,0:T(8,128)} %get-tuple-element.36) | copy-start | bytes 2359300
Sparse Core Ops, SparseCore 0:
  106.5 114.9 all-reduce.8
  224.0 104.8 all-reduce.10
